TPU v7x, 32 devices: a whole 2x2x4 slice. The times are simulated.
32 devices in a mesh: mode: 2 (over x), scan: 16 (over z, y, core).
Axes of the slice: x: 2, y: 2, z: 4, core: 2. Of those that a mesh axis runs over, the one named last changes fastest.
Arguments:
- object_field: float32 [2, 8192, 1024], P(None, 'scan'), may hold values from -4.2 to 4.2
- probe: bfloat16 [2, 12, 512, 512], P(None, 'mode'), may hold values from -1.796875 to 1.796875
- patterns: float32 [16, 512, 512], P('scan'), may hold values from 0.2 to 6
- row_shift: int32 [16], P('scan'), may hold values from 0 to 1
- col_start: int32 [16], P('scan'), may hold values from 0 to 2
- mixing: int32 [12, 12], replicated, may hold values from -5 to 20, as said below
Outputs:
- object_new: float32 [2, 8192, 1024], P(None, 'scan')
- probe_new: bfloat16 [2, 12, 512, 512], P(None, 'mode', 'scan')
Inputs may be any that keep to these rules, and one draw needn't show every extreme that they name: `mixing`: diagonal entries are 12 to 20, the others -5 to 5.
All inputs are finite; a program needn't handle non-finite values.
Results may differ from a plain program's by a relative error of at most 0.0095.
The roundings to bfloat16 on the way count: a program that leaves them out, or rounds other values in their place, can miss the bound.
Values sent between devices are 32-bit elements; how exact they have to be, the bound alone decides.
A program may use at most 128 MiB of HBM per device.

v0:
```python
import math

import jax
import jax.numpy as jnp
from jax import lax
from jax.sharding import PartitionSpec as P


def passed_along(value, axis, steps):
    count = lax.axis_size(axis)
    leading, last = (max(0, -steps), min(count, count - steps))
    return lax.ppermute(value, axis, [(source, source + steps) for source in range(leading, last)])


def tables(tile_size):
    indices = jnp.arange(tile_size, dtype=jnp.int32)
    products = indices[:, None] * indices[None, :] % tile_size
    angles = products.astype(jnp.float32) * (2.0 * math.pi / tile_size)
    factor = 1.0 / math.sqrt(tile_size)
    return (
        (jnp.cos(angles) * factor).astype(jnp.bfloat16),
        (jnp.sin(angles) * factor).astype(jnp.bfloat16),
    )


def right_mult(first, second):
    return jnp.einsum("...ij,jk->...ik", first, second, preferred_element_type=jnp.float32)


def left_mult(first, second):
    return jnp.einsum("ij,...jk->...ik", first, second, preferred_element_type=jnp.float32)


def transform(real_part, imag_part, cosine, sine_table, direction):
    half_real = right_mult(real_part, cosine) - direction * right_mult(imag_part, sine_table)
    half_imag = right_mult(imag_part, cosine) + direction * right_mult(real_part, sine_table)
    half_real = half_real.astype(jnp.bfloat16)
    half_imag = half_imag.astype(jnp.bfloat16)
    out_real = left_mult(cosine, half_real) - direction * left_mult(sine_table, half_imag)
    out_imag = left_mult(cosine, half_imag) + direction * left_mult(sine_table, half_real)
    return (out_real, out_imag)


def per_device(object_field, probe, patterns, row_shift, col_start, mixing):
    tile_size = probe.shape[2]
    half_rows = tile_size // 2
    local_modes = probe.shape[1]
    positions = patterns.shape[0]
    scan_devices = lax.axis_size("scan")
    cosine, sine_table = tables(tile_size)
    lower_rim = passed_along(object_field[:, :half_rows, :], "scan", -1)
    extended = jnp.concatenate([object_field, lower_rim], axis=1)
    zero_index = jnp.zeros((), jnp.int32)
    slot = 0
    row_first = row_shift[slot] * half_rows
    col_first = col_start[slot] * half_rows
    corners = [(row_first, col_first)]
    gathered = [
        lax.dynamic_slice(extended, (zero_index, row_first, col_first), (2, tile_size, tile_size))
    ]
    patches = jnp.stack(gathered, axis=1)
    obj_real = patches[0][:, None]
    obj_imag = patches[1][:, None]
    probe_real = probe[0].astype(jnp.float32)[None]
    probe_imag = probe[1].astype(jnp.float32)[None]
    exit_real = (probe_real * obj_real - probe_imag * obj_imag).astype(jnp.bfloat16)
    exit_imag = (probe_real * obj_imag + probe_imag * obj_real).astype(jnp.bfloat16)
    wave_real, wave_imag = transform(exit_real, exit_imag, cosine, sine_table, -1.0)
    partial_sum = jnp.sum(wave_real * wave_real + wave_imag * wave_imag, axis=1)
    summed = lax.psum(partial_sum, "mode")
    scaling = (jnp.sqrt(patterns) / jnp.sqrt(jnp.maximum(summed, 1.0)))[:, None]
    fixed_real = (wave_real * scaling).astype(jnp.bfloat16)
    fixed_imag = (wave_imag * scaling).astype(jnp.bfloat16)
    back_real, back_imag = transform(fixed_real, fixed_imag, cosine, sine_table, 1.0)
    resid_real = back_real - exit_real.astype(jnp.float32)
    resid_imag = back_imag - exit_imag.astype(jnp.float32)
    grad_real = jnp.sum(probe_real * resid_real + probe_imag * resid_imag, axis=1)
    grad_imag = jnp.sum(probe_real * resid_imag - probe_imag * resid_real, axis=1)
    own_light = jnp.sum(probe_real[0] * probe_real[0] + probe_imag[0] * probe_imag[0], axis=0)
    grad_real, grad_imag, illumination = lax.psum((grad_real, grad_imag, own_light), "mode")
    accum = jnp.zeros((2, tile_size + half_rows, object_field.shape[2]), jnp.float32)
    slot = 0
    row_first, col_first = corners[slot]
    region = jnp.stack([grad_real[slot], grad_imag[slot]])
    accum = lax.dynamic_update_slice(accum, region, (zero_index, row_first, col_first))
    overflow = passed_along(accum[:, tile_size:, :], "scan", 1)
    own_rows = accum[:, :tile_size, :]
    own_rows = own_rows.at[:, :half_rows, :].add(overflow)
    object_new = object_field + own_rows / jnp.max(illumination)
    step_real = jnp.sum(obj_real * resid_real + obj_imag * resid_imag, axis=0)
    step_imag = jnp.sum(obj_real * resid_imag - obj_imag * resid_real, axis=0)
    probe_grad = jnp.stack([step_real, step_imag])
    share_rows = tile_size // scan_devices
    row_start = lax.axis_index("scan") * share_rows
    my_rows = lax.psum_scatter(probe_grad, "scan", scatter_dimension=2, tiled=True)
    probe_rows = lax.dynamic_slice_in_dim(probe, row_start, share_rows, 2).astype(jnp.float32)
    updated = probe_rows + my_rows / math.sqrt(positions * scan_devices)
    everyone = lax.all_gather(updated, "mode", axis=1, tiled=True)
    weights = mixing.astype(jnp.float32) / 16.0
    my_weights = lax.dynamic_slice_in_dim(
        weights, lax.axis_index("mode") * local_modes, local_modes, 0
    )
    probe_new = jnp.einsum("kj,cjrt->ckrt", my_weights, everyone, precision=lax.Precision.HIGHEST)
    return (object_new, probe_new.astype(jnp.bfloat16))


def solution(mesh):
    in_specs = (
        P(None, "scan", None),
        P(None, "mode", None, None),
        P("scan", None, None),
        P("scan"),
        P("scan"),
        P(),
    )
    out_specs = (P(None, "scan", None), P(None, "mode", "scan", None))
    return jax.shard_map(
        per_device, mesh=mesh, in_specs=in_specs, out_specs=out_specs, check_vma=False
    )
```

profile of v0, /device:TPU:0, one launch (start us, length us, event | category | flops | bytes accessed | tf_op | source)
XLA Modules:
  0.0 633.5 jit_solution(16244839592704000290)
XLA Ops:
  7.2 3.2 slice.49
  13.0 5.9 fusion.159
  18.9 3.2 copy.129
  22.1 5.4 copy.130
  36.3 3.9 fusion.3
  40.3 5.0 fusion.16
  45.3 5.0 fusion.18
  50.3 8.3 %add_convert_fusion.1 = bf16[6,512,512]{2,1,0:T(8,128)(2,1)S(1)} fusion(f32[6,512,512]{2,1,0:T(8,128)S(1)} %fusion.16, bf16[1,6,512,512]{2,3,1,0:T(8,128)(2,1)S(1)} %get-tuple-element.34), kind=kOutput, calls=%fused_computation.39 | convolution fusion | flops 1619525632 | bytes 12582912 | tf_op jit(solution)/shard_map/...ij,jk->...ik/dot_general | solution.py:27
  58.7 7.9 %subtract_convert_fusion.1 = bf16[6,512,512]{2,1,0:T(8,128)(2,1)S(1)} fusion(f32[6,512,512]{2,1,0:T(8,128)S(1)} %fusion.18, bf16[1,6,512,512]{2,3,1,0:T(8,128)(2,1)S(1)} %get-tuple-element.34), kind=kOutput, calls=%fused_computation.40 | convolution fusion | flops 1619525632 | bytes 12582912 | tf_op jit(solution)/shard_map/...ij,jk->...ik/dot_general | solution.py:27
  66.6 10.4 %fusion.70 = f32[6,512,512]{2,1,0:T(8,128)S(1)} fusion(bf16[6,512,512]{2,1,0:T(8,128)(2,1)S(1)} %subtract_convert_fusion.1), kind=kOutput, calls=%fused_computation.83 | convolution fusion | flops 1614807040 | bytes 9437184 | tf_op jit(solution)/shard_map/ij,...jk->...ik/dot_general | solution.py:31
  77.0 10.4 %fusion.67 = f32[6,512,512]{2,1,0:T(8,128)S(1)} fusion(bf16[6,512,512]{2,1,0:T(8,128)(2,1)S(1)} %add_convert_fusion.1), kind=kOutput, calls=%fused_computation.82 | convolution fusion | flops 1614807040 | bytes 9437184 | tf_op jit(solution)/shard_map/ij,...jk->...ik/dot_general | solution.py:31
  87.4 13.4 %multiply_subtract_fusion.1 = f32[6,512,512]{2,1,0:T(8,128)S(1)} fusion(f32[6,512,512]{2,1,0:T(8,128)S(1)} %fusion.70, bf16[6,512,512]{2,1,0:T(8,128)(2,1)S(1)} %add_convert_fusion.1), kind=kOutput, calls=%fused_computation.38 | convolution fusion | flops 1617952768 | bytes 15728640 | tf_op jit(solution)/shard_map/ij,...jk->...ik/dot_general | solution.py:31
  100.8 10.6 %fusion.11 = (f32[512,512]{0,1:T(8,128)}, f32[6,512,512]{2,1,0:T(8,128)}) fusion(f32[6,512,512]{2,1,0:T(8,128)S(1)} %multiply_subtract_fusion.1, f32[6,512,512]{2,1,0:T(8,128)S(1)} %fusion.67, bf16[6,512,512]{2,1,0:T(8,128)(2,1)S(1)} %subtract_convert_fusion.1), kind=kOutput, calls=%fused_computation.28 | convolution fusion | flops 1623982080 | bytes 23068672 | tf_op jit(solution)/shard_map/ij,...jk->...ik/dot_general | solution.py:31
  111.8 52.4 %all-reduce.6.cloned.1.call-done = f32[1,512,512]{1,2,0:T(8,128)} async-done(((f32[1,512,512]{1,2,0:T(8,128)}), f32[1,512,512]{1,2,0:T(8,128)}) %all-reduce.6.cloned.1.call-update) | async-done | bytes 1048592 | tf_op jit(solution)/shard_map/psum | solution.py:70
  166.0 8.3 %fusion.49 = f32[6,512,512]{2,1,0:T(8,128)S(1)} fusion(f32[6,512,512]{2,1,0:T(8,128)} %copy-done, f32[512,512]{0,1:T(8,128)S(1)} %multiply_bitcast_fusion), kind=kOutput, calls=%fused_computation.77 | convolution fusion | flops 1617952768 | bytes 13631488 | tf_op jit(solution)/shard_map/...ij,jk->...ik/dot_general | solution.py:27
  174.4 5.4 fusion.45
  179.8 7.9 %add_convert_fusion = bf16[6,512,512]{2,1,0:T(8,128)(2,1)S(1)} fusion(f32[6,512,512]{2,1,0:T(8,128)S(1)} %fusion.45, f32[6,512,512]{2,1,0:T(8,128)S(1)} %bitcast.110, f32[512,512]{0,1:T(8,128)S(1)} %multiply_bitcast_fusion), kind=kOutput, calls=%fused_computation.35 | convolution fusion | flops 1621098496 | bytes 16777216 | tf_op jit(solution)/shard_map/...ij,jk->...ik/dot_general | solution.py:27
  187.7 7.5 %subtract_convert_fusion = bf16[6,512,512]{2,1,0:T(8,128)(2,1)S(1)} fusion(f32[6,512,512]{2,1,0:T(8,128)S(1)} %fusion.49, f32[6,512,512]{2,1,0:T(8,128)S(1)} %bitcast.112, f32[512,512]{0,1:T(8,128)S(1)} %multiply_bitcast_fusion), kind=kOutput, calls=%fused_computation.36 | convolution fusion | flops 1621098496 | bytes 16777216 | tf_op jit(solution)/shard_map/...ij,jk->...ik/dot_general | solution.py:27
  195.1 10.4 %fusion.64 = f32[6,512,512]{2,1,0:T(8,128)S(1)} fusion(bf16[6,512,512]{2,1,0:T(8,128)(2,1)S(1)} %subtract_convert_fusion), kind=kOutput, calls=%fused_computation.81 | convolution fusion | flops 1614807040 | bytes 9437184 | tf_op jit(solution)/shard_map/ij,...jk->...ik/dot_general | solution.py:31
  205.6 10.6 %fusion.61 = f32[6,512,512]{2,1,0:T(8,128)S(1)} fusion(bf16[6,512,512]{2,1,0:T(8,128)(2,1)S(1)} %add_convert_fusion), kind=kOutput, calls=%fused_computation.80 | convolution fusion | flops 1614807040 | bytes 9437184 | tf_op jit(solution)/shard_map/ij,...jk->...ik/dot_general | solution.py:31
  216.2 13.5 %bitcast_subtract_fusion.1 = f32[1,6,512,512]{2,3,1,0:T(8,128)S(1)} fusion(bf16[1,6,512,512]{2,3,1,0:T(8,128)(2,1)S(1)} %copy-done.4, f32[6,512,512]{2,1,0:T(8,128)S(1)} %fusion.64, bf16[6,512,512]{2,1,0:T(8,128)(2,1)S(1)} %add_convert_fusion), kind=kOutput, calls=%fused_computation.24 | convolution fusion | flops 1619525632 | bytes 18874368 | tf_op jit(solution)/shard_map/ij,...jk->...ik/dot_general | solution.py:31
  229.7 16.1 %multiply_add_fusion = (f32[1,6,512,512]{2,3,1,0:T(8,128)}, f32[1,6,512,512]{2,3,1,0:T(8,128)}, f32[512,512]{0,1:T(8,128)}, f32[512,512]{0,1:T(8,128)}, f32[512,512]{0,1:T(8,128)}) fusion(f32[1,6,512,512]{2,3,1,0:T(8,128)S(1)} %bitcast_subtract_fusion.1, f32[512,512]{0,1:T(8,128)} %copy.88, f32[512,512]{0,1:T(8,128)S(1)} %copy-done.8, ...), kind=kOutput, calls=%fused_computation.34 | convolution fusion | flops 1650196480 | bytes 42991616 | tf_op jit(solution)/shard_map/ij,...jk->...ik/dot_general | solution.py:31
  246.1 10.6 %pad_maximum_fusion = f32[2,6,512,512]{2,3,1,0:T(8,128)} fusion(f32[1,6,512,512]{2,3,1,0:T(8,128)} %get-tuple-element.29, f32[1,6,512,512]{2,3,1,0:T(8,128)} %get-tuple-element.28), kind=kLoop, calls=%fused_computation | loop fusion | flops 3145728 | bytes 25165824 | tf_op jit(solution)/shard_map/stack | solution.py:92
  256.7 19.5 %copy.107 = f32[2,6,512,512]{3,0,1,2:T(2,128)} copy(f32[2,6,512,512]{2,3,1,0:T(8,128)} %pad_maximum_fusion) | data formatting | bytes 25165824 | tf_op jit(solution)/shard_map/stack | solution.py:92
  276.3 55.5 %all-reduce.10.cloned.1.call-done = (f32[1,512,512]{1,2,0:T(8,128)}, f32[1,512,512]{1,2,0:T(8,128)}, f32[512,512]{0,1:T(8,128)}) async-done(((f32[1,512,512]{1,2,0:T(8,128)}, f32[1,512,512]{1,2,0:T(8,128)}, f32[512,512]{0,1:T(8,128)}), (f32[1,512,512]{1,2,0:T(8,128)}, f32[1,512,512]{1,2,0:T(8,128)}, f32[512,512]{0,1:T(8,128)})) %all-reduce.10.cloned.1.call-update) | async-done | bytes 3145744 | tf_op jit(solution)/shard_map/psum | solution.py:80
  331.9 3.0 pad_maximum_fusion.1
  345.1 245.2 %all-reduce.8.cloned.1.call-done = f32[2,6,512,512]{3,0,1,2:T(2,128)} async-done(((f32[2,6,512,512]{3,0,1,2:T(2,128)}), f32[2,6,512,512]{3,0,1,2:T(2,128)}) %all-reduce.8.cloned.1.call-update) | async-done | bytes 12582928
  594.1 4.8 slice.58
  599.7 3.6 fusion.29
  603.4 5.8 divide_add_fusion
  609.2 12.2 %all-gather.2.cloned.1.call-done = f32[2,12,32,512]{3,2,0,1:T(8,128)} async-done(((f32[2,6,32,512]{3,2,0,1:T(8,128)}), f32[2,12,32,512]{3,2,0,1:T(8,128)}) %all-gather.2.cloned.1.call-update) | async-done | bytes 1572880 | tf_op jit(solution)/shard_map/all_gather | solution.py:98
  621.4 4.4 fusion.35
  (66 shorter events, 27.5 us)
Async XLA Ops:
  7.2 157.1 %all-reduce.6.cloned.1.call-start = ((), (), s32[]{:S(2)}) async-start(), calls=%async_computation | async-start | bytes 2097152 | tf_op jit(solution)/shard_map/psum | solution.py:70
  10.4 17.2 %collective-permute-start = (f32[2,256,1024]{2,1,0:T(8,128)}, f32[2,256,1024]{2,1,0:T(8,128)}, u32[]{:S(2)}, u32[]{:S(2)}) collective-permute-start(f32[2,256,1024]{2,1,0:T(8,128)} %slice.49), channel_id=1, source_target_pairs={{1,0},{2,1},{3,2},{4,3},{5,4},{6,5},{7,6},{8,7},{9,8},{10,9},{11,1... | collective-permute-start | bytes 6291464 | tf_op jit(solution)/shard_map/ppermute | solution.py:12
  22.1 14.2 %copy-start.5 = (bf16[1,6,512,512]{2,3,1,0:T(8,128)(2,1)}, bf16[1,6,512,512]{2,3,1,0:T(8,128)(2,1)S(1)}, u32[]{:S(2)}) copy-start(bf16[1,6,512,512]{2,3,1,0:T(8,128)(2,1)S(1)} %copy.129) | copy-start | bytes 9437188
  40.2 5.0 copy-start.9
  40.2 18.4 %copy-start.3 = (bf16[1,6,512,512]{2,3,1,0:T(8,128)(2,1)}, bf16[1,6,512,512]{2,3,1,0:T(8,128)(2,1)S(1)}, u32[]{:S(2)}) copy-start(bf16[1,6,512,512]{2,3,1,0:T(8,128)(2,1)S(1)} %get-tuple-element.34) | copy-start | bytes 9437188
  100.8 10.6 %copy-start = (f32[6,512,512]{2,1,0:T(8,128)}, f32[6,512,512]{2,1,0:T(8,128)S(1)}, u32[]{:S(2)}) copy-start(f32[6,512,512]{2,1,0:T(8,128)S(1)} %multiply_subtract_fusion.1) | copy-start | bytes 18874372
  100.8 10.7 %copy-start.11 = (f32[1,512,512]{2,1,0:T(8,128)S(1)}, f32[1,512,512]{2,1,0:T(8,128)}, u32[]{:S(2)}) copy-start(f32[1,512,512]{2,1,0:T(8,128)} %param.10) | copy-start | bytes 3145732
  111.4 220.5 %all-reduce.10.cloned.1.call-start = ((), (), s32[]{:S(2)}) async-start(), calls=%async_computation.3 | async-start | bytes 6291456 | tf_op jit(solution)/shard_map/psum | solution.py:80
  164.2 10.1 %slice-start.2 = ((s8[6291456]{0:T(1024)(128)(4,1)}), s8[4194304]{0:T(1024)(128)(4,1)S(1)}, s32[]{:S(2)}) async-start(s8[6291456]{0:T(1024)(128)(4,1)} %bitcast.111), calls=%async_computation.6 | async-start | bytes 8388608
  166.0 8.4 %slice-start.3 = ((s8[6291456]{0:T(1024)(128)(4,1)}), s8[2097152]{0:T(1024)(128)(4,1)S(1)}, s32[]{:S(2)}) async-start(s8[6291456]{0:T(1024)(128)(4,1)} %bitcast.111), calls=%async_computation.7 | async-start | bytes 4194304
  166.0 13.8 %slice-start = ((s8[6291456]{0:T(1024)(128)(4,1)}), s8[4194304]{0:T(1024)(128)(4,1)S(1)}, s32[]{:S(2)}) async-start(s8[6291456]{0:T(1024)(128)(4,1)} %bitcast.109), calls=%async_computation.4 | async-start | bytes 8388608
  174.3 5.5 slice-start.1
  205.6 10.6 %copy-start.4 = (bf16[1,6,512,512]{2,3,1,0:T(8,128)(2,1)S(1)}, bf16[1,6,512,512]{2,3,1,0:T(8,128)(2,1)}, u32[]{:S(2)}) copy-start(bf16[1,6,512,512]{2,3,1,0:T(8,128)(2,1)} %copy-done.3) | copy-start | bytes 9437188
  216.1 13.6 %copy-start.6 = (bf16[1,6,512,512]{2,3,1,0:T(8,128)(2,1)S(1)}, bf16[1,6,512,512]{2,3,1,0:T(8,128)(2,1)}, u32[]{:S(2)}) copy-start(bf16[1,6,512,512]{2,3,1,0:T(8,128)(2,1)} %copy-done.5) | copy-start | bytes 9437188
  216.1 13.6 %copy-start.7 = (bf16[1,6,512,512]{2,3,1,0:T(8,128)(2,1)S(1)}, bf16[1,6,512,512]{2,3,1,0:T(8,128)(2,1)}, u32[]{:S(2)}) copy-start(bf16[1,6,512,512]{2,3,1,0:T(8,128)(2,1)} %copy.130) | copy-start | bytes 9437188
  216.2 13.6 %copy-start.8 = (f32[512,512]{0,1:T(8,128)S(1)}, f32[512,512]{0,1:T(8,128)}, u32[]{:S(2)}) copy-start(f32[512,512]{0,1:T(8,128)} %copy.86) | copy-start | bytes 3145732
  245.9 344.4 %all-reduce.8.cloned.1.call-start = ((), (), s32[]{:S(2)}) async-start(), calls=%async_computation.2 | async-start | bytes 25165824
  276.3 345.1 %all-gather.2.cloned.1.call-start = ((), (), s32[]{:S(2)}) async-start(), calls=%async_computation.1 | async-start | bytes 2359296 | tf_op jit(solution)/shard_map/all_gather | solution.py:98
  336.8 7.0 %copy-start.13 = (u32[32]{0:T(128)S(1)}, u32[32]{0:T(128)}, u32[]{:S(2)}) copy-start(u32[32]{0:T(128)} %constant.89) | copy-start | bytes 388
  337.9 2.7 copy-start.1
  342.1 257.6 %collective-permute-start.1 = (f32[2,256,1024]{2,1,0:T(8,128)}, f32[2,256,1024]{2,1,0:T(8,128)S(1)}, u32[]{:S(2)}, u32[]{:S(2)}) collective-permute-start(f32[2,256,1024]{2,1,0:T(8,128)} %slice.60), channel_id=1, source_target_pairs={{0,1},{1,2},{2,3},{3,4},{4,5},{5,6},{6,7},{7,8},{8,9},{9,10},{10,1... | collective-permute-start | bytes 6291464 | tf_op jit(solution)/shard_map/ppermute | solution.py:12
  591.7 7.1 %copy-start.10 = (f32[512,512]{0,1:T(8,128)S(1)}, f32[512,512]{0,1:T(8,128)}, u32[]{:S(2)}) copy-start(f32[512,512]{0,1:T(8,128)} %get-tuple-element.27) | copy-start | bytes 3145732
  599.7 3.6 copy-start.2
  603.4 18.1 %copy-start.12 = (s32[12,12]{1,0:T(8,128)S(1)}, s32[12,12]{1,0:T(8,128)}, u32[]{:S(2)}) copy-start(s32[12,12]{1,0:T(8,128)} %param.13) | copy-start | bytes 1732
Sparse Core Ops, SparseCore 0:
  111.5 52.6 all-reduce.5
  246.0 85.8 all-reduce.9
  335.7 254.5 all-reduce.7
  594.2 27.2 all-gather.1
where the time goes:
time: 638 us; the launch traced here: 633 us
  waiting for transfers between devices  366 us (57%)
  matrix products  155 us (24%)
  local copies, waits for them, and re-layouts  60 us (9%)
  other arithmetic  33.1 us (5%)
  between operations  16.3 us (3%)
    unnamed x5, waiting for transfers between devices  245 us
    dot_general x8, matrix products, left_mult(): jnp.einsum('ij,...jk->...ik', first, second, preferred_element_type=jnp.f...  95.4 us
    psum x1, waiting for transfers between devices, per_device(): lax.psum((grad_real, grad_imag, own_light), 'mode')  55.5 us
    dot_general x8, matrix products, right_mult(): jnp.einsum('...ij,jk->...ik', first, second, preferred_element_type=jnp.f...  55.3 us
    psum x1, waiting for transfers between devices, per_device(): summed = lax.psum(partial_sum, 'mode')  52.4 us
    another operation x1, local copies, waits for them, and re-layouts, per_device(): probe_grad = jnp.stack([step_real, step_imag])  19.5 us
    unnamed x42, local copies, waits for them, and re-layouts  14.6 us
  transfers between devices with their start and end apart: 6, of which 4 were waited for; matrix products, arithmetic and copies ran while one was open for 11% of the time, Pallas kernels for 0%

commit v1 on v0

v1 whole, which is shorter than its diff:
```python
import functools
import math

import jax
import jax.numpy as jnp
import numpy as np
from jax import lax
from jax.experimental import pallas as pl
from jax.experimental.pallas import tpu as pltpu
from jax.sharding import PartitionSpec as P

BF16 = jnp.bfloat16
F32 = jnp.float32


def tables(tile_size):
    indices = np.arange(tile_size)
    products = indices[:, None] * indices[None, :] % tile_size
    angles = products * (2.0 * math.pi / tile_size)
    factor = 1.0 / math.sqrt(tile_size)
    cosine = (np.cos(angles).astype(np.float32) * np.float32(factor)).astype(BF16)
    sine = (np.sin(angles).astype(np.float32) * np.float32(factor)).astype(BF16)
    return cosine, sine


def kernel(
    dims,
    shift_ref, col_ref, mix_ref,
    obj, probe, rows_in, pat, cos_t, sin_t,
    delta, probe_new,
    rim, patch, t1, t2, half, big, recv1, recv2, recv3,
    light, light_in, own_sum, peer_sum, down_in, upd, upd_in, lmax,
    rim_sem, light_sem, sum_sem, sem1, sem2, sem3, sem4, down_sem, out_sem, table_sem,
):
    n, group, share, tile, modes, positions, cols = dims
    hb = tile // 2
    quarter = tile // 4
    me = lax.axis_index("mode")
    idx = lax.axis_index("scan")
    a = idx % 2
    b = (idx // 2) % 2
    m = idx // 4
    other = 1 - me
    sib = idx + 1 - 2 * a
    yid = idx + 2 - 4 * b
    nxt = (idx + 1) % n
    prv = (idx + n - 1) % n

    def remote(src, dst, sems, mode, scan):
        return pltpu.make_async_remote_copy(
            src_ref=src, dst_ref=dst, send_sem=sems[0], recv_sem=sems[1],
            device_id=(mode, scan), device_id_type=pl.DeviceIdType.MESH,
        )

    front, back = pl.ds(0, tile), pl.ds(tile, tile)
    table_copies = [
        pltpu.make_async_copy(cos_t, t1.at[front, front], table_sem.at[0]),
        pltpu.make_async_copy(cos_t, t1.at[back, back], table_sem.at[1]),
        pltpu.make_async_copy(sin_t, t1.at[back, front], table_sem.at[2]),
    ]
    for copy in table_copies:
        copy.start()

    partners = [(other, idx), (me, sib), (me, yid), (me, nxt), (me, prv)]
    partners += [(me, ((m + j) % group) * 4 + b * 2 + a) for j in range(1, group)]
    barrier = pltpu.get_barrier_semaphore()
    for partner in partners:
        pl.semaphore_signal(barrier, inc=1, device_id=partner, device_id_type=pl.DeviceIdType.MESH)
    pl.semaphore_wait(barrier, len(partners))

    rim_copy = remote(obj.at[:, pl.ds(0, hb), :], rim, (rim_sem.at[0], rim_sem.at[1]), me, prv)
    rim_copy.start()

    for h in range(2):
        rs = pl.ds(h * hb, hb)
        light[0, rs, :] = jnp.zeros((hb, tile), F32)

        def add_light(k, carry):
            pr = probe[0, k, rs, :].astype(F32)
            pi = probe[1, k, rs, :].astype(F32)
            light[0, rs, :] = light[0, rs, :] + (pr * pr + pi * pi)
            return carry

        lax.fori_loop(0, modes, add_light, 0)
    light_copy = remote(
        light.at[0], light_in.at[0], (light_sem.at[0], light_sem.at[1]), other, idx
    )
    light_copy.start()

    for copy in table_copies:
        copy.wait()
    t1[0:tile, tile:] = -t1[tile:, 0:tile]
    t2[0:tile, 0:tile] = t1[0:tile, 0:tile]
    t2[0:tile, tile:] = t1[tile:, 0:tile]
    t2[tile:, 0:tile] = t1[0:tile, tile:]
    t2[tile:, tile:] = t1[0:tile, 0:tile]

    col = col_ref[0]
    moved = shift_ref[0].astype(F32)
    stays = 1.0 - moved
    halves = cols // hb
    strip = 32

    def hit(value, q):
        return jnp.maximum(1 - (value - q) * (value - q), 0)

    at_col = [hit(col, q).astype(F32) for q in range(halves - 1)]

    def window(ref, c, first):
        total = at_col[0] * ref[c, pl.ds(first, strip), pl.ds(0, tile)]
        for q in range(1, halves - 1):
            total = total + at_col[q] * ref[c, pl.ds(first, strip), pl.ds(q * hb, tile)]
        return total

    def exits(k, rs):
        pr = probe[0, k, rs, :].astype(F32)
        pi = probe[1, k, rs, :].astype(F32)
        o_r = patch[0, rs, :]
        o_i = patch[1, rs, :]
        er = (pr * o_r - pi * o_i).astype(BF16)
        ei = (pr * o_i + pi * o_r).astype(BF16)
        return pr, pi, o_r, o_i, er, ei

    for h in range(2):
        rs = pl.ds(h * hb, hb)
        if h == 1:
            rim_copy.wait()

        def gather(i, carry):
            here = pl.multiple_of(i * strip, strip)
            for c in range(2):
                if h == 0:
                    low = window(obj, c, hb + here)
                    top = window(obj, c, here)
                else:
                    low = jnp.where(idx == n - 1, 0.0, window(rim, c, here))
                    top = window(obj, c, hb + here)
                patch[c, pl.ds(h * hb + here, strip), :] = moved * low + stays * top
            return carry

        lax.fori_loop(0, hb // strip, gather, 0)

        def right(k, carry):
            er, ei = exits(k, rs)[4:]
            out = jnp.dot(
                jnp.concatenate([er, ei], axis=1), t1[...], preferred_element_type=F32
            ).astype(BF16)
            half[k, pl.ds(h * hb, hb), :] = out[:, :tile]
            half[k, pl.ds(tile + h * hb, hb), :] = out[:, tile:]
            return carry

        lax.fori_loop(0, modes, right, 0)

    light_copy.wait()
    lmax[...] = jnp.full(lmax.shape, jnp.max(light[0] + light_in[0]), F32)

    sum_copies = []
    for h in range(2):
        own_sum[h, 0:hb] = jnp.zeros((hb, tile), F32)

        def left(k, carry):
            wr = jnp.dot(t2[pl.ds(h * hb, hb), :], half[k], preferred_element_type=F32)
            wi = jnp.dot(t2[pl.ds(tile + h * hb, hb), :], half[k], preferred_element_type=F32)
            own_sum[h, 0:hb] = own_sum[h, 0:hb] + (wr * wr + wi * wi)
            for q in range(2):
                big[k, h, q, 0] = wr[q * quarter:(q + 1) * quarter].reshape(group, share, tile)
                big[k, h, q, 1] = wi[q * quarter:(q + 1) * quarter].reshape(group, share, tile)
            return carry

        lax.fori_loop(0, modes, left, 0)
        copy = remote(
            own_sum.at[h, pl.ds(0, hb)], peer_sum.at[h], (sum_sem.at[0, h], sum_sem.at[1, h]), other, idx
        )
        copy.start()
        sum_copies.append(copy)

    for h in range(2):
        sum_copies[h].wait()
        rs = pl.ds(h * hb, hb)
        total = jnp.maximum(own_sum[h, 0:hb] + peer_sum[h], 1.0)
        own_sum[h, 0:hb] = jnp.sqrt(pat[0, rs, :]) / jnp.sqrt(total)

        def fix(k, carry):
            scale = own_sum[h, 0:hb]
            parts = []
            for c in range(2):
                w = jnp.concatenate(
                    [big[k, h, q, c].reshape(quarter, tile) for q in range(2)], axis=0
                )
                parts.append((w * scale).astype(BF16))
            out = jnp.dot(
                jnp.concatenate(parts, axis=1), t2[...], preferred_element_type=F32
            ).astype(BF16)
            half[k, pl.ds(h * hb, hb), :] = out[:, :tile]
            half[k, pl.ds(tile + h * hb, hb), :] = out[:, tile:]
            return carry

        lax.fori_loop(0, modes, fix, 0)

    light[...] = jnp.zeros(light.shape, F32)

    def copy1(k):
        return remote(big.at[k, 1 - a], recv1.at[k], (sem1.at[0, k], sem1.at[1, k]), me, sib)

    def copy2(k):
        return remote(big.at[k, a, 1 - b], recv2.at[k], (sem2.at[0, k], sem2.at[1, k]), me, yid)

    def copy3(k, j):
        to = (m + j) % group
        return remote(
            big.at[k, a, b, :, to], recv3.at[k, j - 1],
            (sem3.at[0, k, j - 1], sem3.at[1, k, j - 1]), me, to * 4 + b * 2 + a,
        )

    def copy4(k):
        return remote(upd.at[k], upd_in.at[k], (sem4.at[0, k], sem4.at[1, k]), other, idx)

    def stage2(k):
        copy1(k).wait()
        big[k, a, 1 - b] = big[k, a, 1 - b] + recv1[k, 1 - b]
        copy2(k).start()
        big[k, a, b] = big[k, a, b] + recv1[k, b]

    def stage3(k):
        copy2(k).wait()
        big[k, a, b] = big[k, a, b] + recv2[k]
        for j in range(1, group):
            copy3(k, j).start()

    def stage4(k):
        total = big[k, a, b, :, m]
        for j in range(1, group):
            copy3(k, j).wait()
            total = total + recv3[k, j - 1]
        upd[k] = rows_in[k].astype(F32) + total / math.sqrt(positions)
        copy4(k).start()

    def step(k, carry):
        for h in range(2):
            rs = pl.ds(h * hb, hb)
            pr, pi, o_r, o_i, er, ei = exits(k, rs)
            rr = jnp.dot(t1[rs, :], half[k], preferred_element_type=F32) - er.astype(F32)
            ri = jnp.dot(
                t1[pl.ds(tile + h * hb, hb), :], half[k], preferred_element_type=F32
            ) - ei.astype(F32)
            light[0, rs, :] = light[0, rs, :] + (pr * rr + pi * ri)
            light[1, rs, :] = light[1, rs, :] + (pr * ri - pi * rr)
            grads = (o_r * rr + o_i * ri, o_r * ri - o_i * rr)
            for c in range(2):
                g = grads[c].reshape(group // 2, 2, 2, share, tile)
                for qb in range(2):
                    for qa in range(2):
                        big[k, qa, qb, c, pl.ds(h * (group // 2), group // 2)] = g[:, qb, qa]
        copy1(k).start()

        @pl.when(k >= 1)
        def _():
            stage2(k - 1)

        @pl.when(k >= 3)
        def _():
            stage3(k - 3)

        return carry

    lax.fori_loop(0, modes, step, 0)
    grad_copy = remote(light, light_in, (light_sem.at[2], light_sem.at[3]), other, idx)
    grad_copy.start()
    stage2(modes - 1)

    def drain(k, carry):
        stage3(k)
        stage4(k - modes + 3)
        return carry

    lax.fori_loop(modes - 3, modes, drain, 0)

    grad_copy.wait()
    light[...] = light[...] + light_in[...]
    own_sum[:, pl.ds(0, hb), :] = moved * light[:, pl.ds(hb, hb), :]
    own_sum[:, pl.ds(hb, 8), :] = jnp.full((2, 8, tile), col.astype(F32), F32)
    down_copy = remote(own_sum, down_in, (down_sem.at[0], down_sem.at[1]), me, nxt)
    down_copy.start()

    def finish(k, carry):
        stage4(k)
        return carry

    lax.fori_loop(3, modes, finish, 0)

    down_copy.wait()
    out_copies = []
    for c in range(2):
        for h in range(2):
            for z in range(2):
                rs = pl.ds(z * quarter, quarter)
                first = light[c, rs, :]
                if h == 0:
                    piece = stays * first / lmax[0:1, 0:1]
                    near = jnp.where(idx == 0, 0.0, down_in[c, rs, :]) / lmax[0:1, 0:1]
                    ncol = down_in[c, pl.ds(hb, 1), pl.ds(0, hb)]
                else:
                    second = light[c, pl.ds(hb + z * quarter, quarter), :]
                    piece = (stays * second + moved * first) / lmax[0:1, 0:1]
                for q in range(halves):
                    value = jnp.zeros((quarter, hb), F32)
                    if q < halves - 1:
                        value = at_col[q] * piece[:, :hb]
                        if h == 0:
                            value = value + hit(ncol, float(q)) * near[:, :hb]
                    if q > 0:
                        value = value + at_col[q - 1] * piece[:, hb:]
                        if h == 0:
                            value = value + hit(ncol, float(q - 1)) * near[:, hb:]
                    big[q // 2, h, z, c, :, :, pl.ds((q % 2) * hb, hb)] = value.reshape(
                        group, share, hb
                    )
            for z in range(2):
                for w in range(cols // tile):
                    copy = pltpu.make_async_copy(
                        big.at[w, h, z, c],
                        delta.at[c, pl.ds((h * 2 + z) * group, group), :, pl.ds(w * tile, tile)],
                        out_sem.at[c, h, z, w],
                    )
                    copy.start()
                    out_copies.append(copy)

    def arrived(k, carry):
        copy4(k).wait()
        return carry

    lax.fori_loop(0, modes, arrived, 0)
    for k in range(modes):
        acc = jnp.zeros((2, share, tile), F32)
        for j in range(modes):
            own = mix_ref[me * modes + k, me * modes + j].astype(F32) / 16.0
            far = mix_ref[me * modes + k, other * modes + j].astype(F32) / 16.0
            acc = acc + own * upd[j] + far * upd_in[j]
        for c in range(2):
            probe_new[c, k] = acc[c].astype(BF16)
    for copy in out_copies:
        copy.wait()


def per_device(object_field, probe, patterns, row_shift, col_start, mixing):
    tile = probe.shape[2]
    modes = probe.shape[1]
    cols = object_field.shape[2]
    n = lax.axis_size("scan")
    group = n // 4
    share = tile // n
    positions = patterns.shape[0] * n
    cosine, sine = tables(tile)
    hb = tile // 2
    dims = (n, group, share, tile, modes, positions, cols)
    row_start = lax.axis_index("scan") * share
    rows_in = lax.dynamic_slice_in_dim(probe, row_start, share, 2).transpose(1, 0, 2, 3)
    smem = pl.BlockSpec(memory_space=pltpu.SMEM)
    vmem = pl.BlockSpec(memory_space=pltpu.VMEM)
    dma = pltpu.SemaphoreType.DMA
    delta, probe_new = pl.pallas_call(
        functools.partial(kernel, dims),
        out_shape=(
            jax.ShapeDtypeStruct((2, tile // share, share, cols), F32),
            jax.ShapeDtypeStruct((2, modes, share, tile), BF16),
        ),
        in_specs=[smem, smem, smem] + [vmem] * 4 + [pl.BlockSpec(memory_space=pl.ANY)] * 2,
        out_specs=(pl.BlockSpec(memory_space=pl.ANY), vmem),
        scratch_shapes=[
            pltpu.VMEM((2, hb, cols), F32),
            pltpu.VMEM((2, tile, tile), F32),
            pltpu.VMEM((2 * tile, 2 * tile), BF16),
            pltpu.VMEM((2 * tile, 2 * tile), BF16),
            pltpu.VMEM((modes, 2 * tile, tile), BF16),
            pltpu.VMEM((modes, 2, 2, 2, group, share, tile), F32),
            pltpu.VMEM((modes, 2, 2, group, share, tile), F32),
            pltpu.VMEM((modes, 2, group, share, tile), F32),
            pltpu.VMEM((modes, group - 1, 2, share, tile), F32),
            pltpu.VMEM((2, tile, tile), F32),
            pltpu.VMEM((2, tile, tile), F32),
            pltpu.VMEM((2, hb + 8, tile), F32),
            pltpu.VMEM((2, hb, tile), F32),
            pltpu.VMEM((2, hb + 8, tile), F32),
            pltpu.VMEM((modes, 2, share, tile), F32),
            pltpu.VMEM((modes, 2, share, tile), F32),
            pltpu.VMEM((8, 128), F32),
            dma((2,)),
            dma((4,)),
            dma((2, 2)),
            dma((2, modes)),
            dma((2, modes)),
            dma((2, modes, group - 1)),
            dma((2, modes)),
            dma((2,)),
            dma((2, 2, 2, cols // tile)),
            dma((3,)),
        ],
        compiler_params=pltpu.CompilerParams(
            collective_id=0, has_side_effects=True, vmem_limit_bytes=67_000_000
        ),
    )(row_shift, col_start, mixing, object_field, probe, rows_in, patterns, cosine, sine)
    return (object_field + delta.reshape(object_field.shape), probe_new)


def solution(mesh):
    in_specs = (
        P(None, "scan", None),
        P(None, "mode", None, None),
        P("scan", None, None),
        P("scan"),
        P("scan"),
        P(),
    )
    out_specs = (P(None, "scan", None), P(None, "mode", "scan", None))
    return jax.shard_map(
        per_device, mesh=mesh, in_specs=in_specs, out_specs=out_specs, check_vma=False
    )
```

time: 638 us -> 191 us (0.30)
  waiting for transfers between devices: 366 us -> 0 us
  Pallas kernels: 0 us -> 179 us
  matrix products: 155 us -> 0 us
  local copies, waits for them, and re-layouts: 60 us -> 2.53 us
  other arithmetic: 33.1 us -> 6.88 us
  between operations: 16.3 us -> 1.94 us
    unnamed x5 -> x0, waiting for transfers between devices: 245 us -> none
    pallas_call x0 -> x1, Pallas kernels: none -> 179 us  [per_device(): pl.pallas_call(functools.partial(kernel, dims), out_shape=(jax.ShapeDtype...]
    dot_general x17 -> x0, matrix products: 155 us -> none  [the longest x8 95.4 us: left_mult(): jnp.einsum('ij,...jk->...ik', first, second, preferred_element_type=jnp.f...]
    psum x2 -> x0, waiting for transfers between devices: 108 us -> none  [the longest x1 55.5 us: per_device(): lax.psum((grad_real, grad_imag, own_light), 'mode')]
    another operation x2 -> x0, local copies, waits for them, and re-layouts: 21.5 us -> none  [the longest x1 19.5 us: per_device(): probe_grad = jnp.stack([step_real, step_imag])]
    slice x4 -> x0, local copies, waits for them, and re-layouts: 15.4 us -> none  [the longest x1 5.93 us: per_device(): probe_imag = probe[1].astype(jnp.float32)[None]]
    unnamed x42 -> x3, local copies, waits for them, and re-layouts: 14.6 us -> 0.75 us
    another operation x2 -> x0, other arithmetic: 13.6 us -> none  [the longest x1 10.6 us: per_device(): probe_grad = jnp.stack([step_real, step_imag])]
  transfers between devices with their start and end apart: 6 -> 0, of which waited for: 4 -> 0; matrix products, arithmetic and copies ran while one was open for 11% -> 0% of each run, Pallas kernels for 0% -> 0%
where the time goes in v1:
time: 191 us; the launch traced here: 190 us
  Pallas kernels  179 us (94%)
  other arithmetic  6.88 us (4%)
  local copies, waits for them, and re-layouts  2.53 us (1%)
  between operations  1.94 us (1%)
    pallas_call x1, Pallas kernels, per_device(): pl.pallas_call(functools.partial(kernel, dims), out_shape=(jax.ShapeDtype...  179 us
    add x1, other arithmetic, per_device(): return (object_field + delta.reshape(object_field.shape), probe_new)  6.88 us

profile of v1, /device:TPU:0, one launch (start us, length us, event | category | flops | bytes accessed | tf_op | source)
XLA Modules:
  0.0 190.4 jit_solution(689849711819029760)
XLA Ops:
  1.9 1.8 copy_bitcast_fusion.rows_in
  3.7 179.1 %shard_map.95 = (f32[2,16,32,1024]{3,2,1,0:T(8,128)}, bf16[2,6,32,512]{3,2,1,0:T(8,128)(2,1)}) custom-call(s32[1]{0:T(128)S(6)} %copy.14.shift_ref, s32[1]{0:T(128)S(6)} %copy.15.col_ref, s32[12,12]{1,0:T(8,128)} %mix_ref.1, f32[2,512,1024]{2,1,0:T(8,128)} %obj.1, bf16[2,6,512,512]{3,2,1,0:T(8,128)(2,1)} %probe.1, ...), custom_call_target="tpu_custom_call" | custom-call | tf_op jit(solution)/shard_map/pallas_call | solution.py:361
  182.8 0.0 copy-start
  182.8 6.9 %bitcast_add_fusion = f32[2,512,1024]{2,1,0:T(8,128)} fusion(f32[2,512,1024]{2,1,0:T(8,128)} %obj.1, f32[2,16,32,1024]{3,2,1,0:T(8,128)} %get-tuple-element.4), kind=kLoop, calls=%fused_computation | loop fusion | flops 1048576 | bytes 12582912 | tf_op jit(solution)/shard_map/add | solution.py:402
  189.7 0.0 copy-done
  189.7 0.7 copy.16
Async XLA Ops:
  182.8 6.9 %copy-start = (bf16[2,6,32,512]{3,2,1,0:T(8,128)(2,1)S(1)}, bf16[2,6,32,512]{3,2,1,0:T(8,128)(2,1)}, u32[]{:S(2)}) copy-start(bf16[2,6,32,512]{3,2,1,0:T(8,128)(2,1)} %get-tuple-element.9) | copy-start | bytes 1179652
